TPU v7x, 32 devices: a whole 2x2x4 slice. The times are simulated.
32 devices in a mesh: groups: 2 (over y), section: 4 (over z), dp: 4 (over x, core).
Axes of the slice: x: 2, y: 2, z: 4, core: 2. Of those that a mesh axis runs over, the one named last changes fastest.
Arguments:
- stream_in: bfloat16 [1152, 3072], P(('groups', 'dp')), parts along dimension 0, may hold values from -6 to 6
- out_grad: bfloat16 [1152, 3072], P(('groups', 'dp')), parts along dimension 0, may hold values from -6 to 6
- mask_blocks: int32 [24, 3, 3], P(('groups', 'dp')), parts along dimension 0, may hold values from 0 to 2, as said below
- norm_gain: float32 [4, 3072], P('section'), may hold values from 0.4 to 1.6
- w_joined: bfloat16 [4, 3072, 1664], P('section', 'dp'), may hold values from -0.109375 to 0.109375
- w_out: bfloat16 [4, 1536, 3072], P('section', 'dp'), may hold values from -0.15625 to 0.15625
Outputs:
- grad_joined: float32 [8, 3072, 1664], P(('groups', 'section'), 'dp'), parts along dimension 0
- grad_out: float32 [8, 1536, 3072], P(('groups', 'section'), 'dp'), parts along dimension 0
- gain_grad: float32 [8, 3072], P(('groups', 'section')), parts along dimension 0
There are 2 independent parts, one for each index of `groups`. A program takes and returns all parts, laid end to end along the dimension named above; an argument that names none is the same for every part. Nothing has to cross between parts.
Inputs may be any that keep to these rules, and one draw needn't show every extreme that they name: `mask_blocks`: entry 0 of the list of query block i is i itself.
All inputs are finite; a program needn't handle non-finite values.
Results may differ from a plain program's by a relative error of at most 0.024.
Values may be sent and summed in bfloat16 or wider, within the bound.
A program may use at most 128 MiB of HBM per device.

v0:
```python
import jax
import jax.numpy as jnp
from jax import lax
from jax.sharding import PartitionSpec as P

NUM_HEADS = 24
HEAD_DIM = 64
BLOCK_LEN = 16
EPSILON = 1e-05


def from_behind(value, axis, steps):
    count = lax.axis_size(axis)
    initial, last = (max(0, -steps), min(count, count - steps))
    return lax.ppermute(value, axis, [(source, source + steps) for source in range(initial, last)])


def allowed_tokens(links, block_len):
    count = links.shape[1]
    block_hits = links[:, :, :, None] == jnp.arange(count, dtype=jnp.int32)[None, None, None, :]
    blocks = jnp.any(block_hits, axis=2)
    return jnp.repeat(jnp.repeat(blocks, block_len, axis=1), block_len, axis=2)


def normalize(stream, gain_row):
    stream_wide = stream.astype(jnp.float32)
    inv_rms = lax.rsqrt(jnp.mean(stream_wide * stream_wide, axis=-1, keepdims=True) + EPSILON)
    normed = (stream_wide * inv_rms * gain_row).astype(jnp.bfloat16)
    return (stream_wide, inv_rms, normed)


def project(normed, weight):
    batch_size, length, model_width = normed.shape
    flat = jnp.dot(normed.reshape(-1, model_width), weight, preferred_element_type=jnp.float32)
    return flat.astype(jnp.bfloat16).reshape(batch_size, length, weight.shape[1])


def attend(joined_rows, allowed):
    batch_size, length, _ = joined_rows.shape
    inner_width = NUM_HEADS * HEAD_DIM
    queries = joined_rows[:, :, :inner_width].reshape(batch_size, length, NUM_HEADS, HEAD_DIM)
    key_rows = joined_rows[:, :, inner_width : inner_width + HEAD_DIM]
    values = joined_rows[:, :, inner_width + HEAD_DIM :]
    scores = jnp.einsum(
        "bihd,bjd->bhij", queries, key_rows, preferred_element_type=jnp.float32
    ) * HEAD_DIM ** (-0.5)
    scores = jnp.where(allowed[:, None], scores, -1e30)
    row_max = jnp.max(scores, axis=-1, keepdims=True)
    exp_scores = jnp.exp(scores - row_max)
    attn_probs = exp_scores / jnp.sum(exp_scores, axis=-1, keepdims=True)
    probs_half = attn_probs.astype(jnp.bfloat16)
    mixed_heads = jnp.einsum(
        "bhij,bjd->bihd", probs_half, values, preferred_element_type=jnp.float32
    )
    mixed_heads = mixed_heads.astype(jnp.bfloat16).reshape(batch_size, length, inner_width)
    return (queries, key_rows, values, attn_probs, probs_half, mixed_heads)


def layer_forward(stream, gain_row, w_joined, w_out, allowed):
    stream_wide, inv_rms, normed = normalize(stream, gain_row)
    joined_rows = project(normed, w_joined)
    _, _, _, attn_probs, _, mixed_heads = attend(joined_rows, allowed)
    batch_size, length, model_width = stream.shape
    update = jnp.dot(
        mixed_heads.reshape(-1, mixed_heads.shape[2]), w_out, preferred_element_type=jnp.float32
    )
    result = (stream_wide + update.reshape(batch_size, length, model_width)).astype(jnp.bfloat16)
    return (result, normed, joined_rows, attn_probs, mixed_heads)


def layer_backward(stream, gain_row, joined_rows, attn_probs, w_joined, w_out, upstream):
    batch_size, length, model_width = stream.shape
    inner_width = NUM_HEADS * HEAD_DIM
    stream_wide = stream.astype(jnp.float32)
    inv_rms = lax.rsqrt(jnp.mean(stream_wide * stream_wide, axis=-1, keepdims=True) + EPSILON)
    queries = joined_rows[:, :, :inner_width].reshape(batch_size, length, NUM_HEADS, HEAD_DIM)
    key_rows = joined_rows[:, :, inner_width : inner_width + HEAD_DIM]
    values = joined_rows[:, :, inner_width + HEAD_DIM :]
    probs_half = attn_probs.astype(jnp.bfloat16)
    grad_mixed = lax.dot_general(
        upstream.reshape(-1, model_width),
        w_out,
        (((1,), (1,)), ((), ())),
        preferred_element_type=jnp.float32,
    )
    grad_mixed = grad_mixed.astype(jnp.bfloat16).reshape(batch_size, length, NUM_HEADS, HEAD_DIM)
    grad_probs = jnp.einsum(
        "bihd,bjd->bhij", grad_mixed, values, preferred_element_type=jnp.float32
    )
    grad_values = jnp.einsum(
        "bhij,bihd->bjd", probs_half, grad_mixed, preferred_element_type=jnp.float32
    )
    inner_sum = jnp.sum(attn_probs * grad_probs, axis=-1, keepdims=True)
    grad_scores = (attn_probs * (grad_probs - inner_sum) * HEAD_DIM ** (-0.5)).astype(jnp.bfloat16)
    grad_queries = jnp.einsum(
        "bhij,bjd->bihd", grad_scores, key_rows, preferred_element_type=jnp.float32
    )
    grad_keys = jnp.einsum(
        "bhij,bihd->bjd", grad_scores, queries, preferred_element_type=jnp.float32
    )
    grad_joined_rows = jnp.concatenate(
        [grad_queries.reshape(batch_size, length, inner_width), grad_keys, grad_values], axis=-1
    ).astype(jnp.bfloat16)
    grad_normed = lax.dot_general(
        grad_joined_rows.reshape(-1, grad_joined_rows.shape[2]),
        w_joined,
        (((1,), (1,)), ((), ())),
        preferred_element_type=jnp.float32,
    )
    grad_normed = grad_normed.reshape(batch_size, length, model_width)
    gained = grad_normed * gain_row
    grad_stream = inv_rms * gained - stream_wide * inv_rms**3 * jnp.mean(
        stream_wide * gained, axis=-1, keepdims=True
    )
    down_grad = (upstream.astype(jnp.float32) + grad_stream).astype(jnp.bfloat16)
    gain_part = jnp.sum((grad_normed * stream_wide * inv_rms).reshape(-1, model_width), axis=0)
    return (down_grad, grad_joined_rows, gain_part)


def pick(stack, index):
    return lax.dynamic_index_in_dim(stack, index, 0, keepdims=False)


def gather_weights(w_joined, w_out):
    return (
        lax.all_gather(w_joined[0], "dp", axis=0, tiled=True),
        lax.all_gather(w_out[0], "dp", axis=0, tiled=True),
    )


def share_columns(rows):
    n = lax.axis_size("dp")
    me = lax.axis_index("dp")
    slots, length, total = rows.shape
    width = total // n
    taken = jnp.zeros((slots, n, length, width), rows.dtype)
    for shift in range(n):
        target = lax.rem(me + shift, n)
        piece = lax.dynamic_slice_in_dim(rows, target * width, width, 2)
        if shift:
            piece = lax.ppermute(piece, "dp", [(i, (i + shift) % n) for i in range(n)])
        source = lax.rem(me + n - shift, n)
        taken = lax.dynamic_update_slice_in_dim(taken, piece[:, None], source, 1)
    return taken


def body(stream_in, out_grad, mask_blocks, norm_gain, w_joined, w_out):
    full_joined, full_out = gather_weights(w_joined, w_out)
    gain_row = norm_gain[0]
    sections = lax.axis_size("section")
    section_index = lax.axis_index("section")
    micro_count = mask_blocks.shape[0]
    model_width = stream_in.shape[1]
    length = stream_in.shape[0] // micro_count
    inputs = stream_in.reshape(micro_count, 1, length, model_width)
    upstreams = out_grad.reshape(micro_count, 1, length, model_width)
    allowed = allowed_tokens(mask_blocks, BLOCK_LEN).reshape(micro_count, 1, length, length)
    step_count = micro_count + sections - 1

    def forward_step(step, state):
        incoming, kept = state
        slot = step - section_index
        active = jnp.logical_and(slot >= 0, slot < micro_count)
        group_index = jnp.clip(slot, 0, micro_count - 1)
        source = jnp.where(section_index == 0, pick(inputs, group_index), incoming)
        result, normed, joined_rows, attn_probs, mixed_heads = layer_forward(
            source, gain_row, full_joined, full_out, pick(allowed, group_index)
        )
        place = jnp.where(active, group_index, micro_count)
        values = (source, joined_rows, attn_probs, normed, mixed_heads)
        kept = tuple(
            (
                lax.dynamic_update_index_in_dim(store, value, place, 0)
                for store, value in zip(kept, values)
            )
        )
        return (from_behind(result, "section", 1), kept)

    def store_of(*shape, dtype=jnp.bfloat16):
        return jnp.zeros((micro_count + 1,) + shape, dtype)

    joined_width = full_joined.shape[1]
    inner_width = full_out.shape[0]
    rest = jnp.zeros((1, length, model_width), jnp.bfloat16)
    kept = (
        store_of(1, length, model_width),
        store_of(1, length, joined_width),
        store_of(1, NUM_HEADS, length, length, dtype=jnp.float32),
        store_of(1, length, model_width),
        store_of(1, length, inner_width),
    )
    _, kept = lax.fori_loop(0, step_count, forward_step, (rest, kept))
    sources, joineds, probs, normeds, mixeds = kept
    columns_normed = share_columns(normeds[:micro_count, 0])
    columns_mixed = share_columns(mixeds[:micro_count, 0])
    behind = sections - 1 - section_index
    replicas = lax.axis_size("dp")

    def place_of(slot):
        return jnp.where(jnp.logical_and(slot >= 0, slot < micro_count), slot, micro_count)

    def backward_step(step, state):
        incoming, last_rows, all_upstream, all_joined, gain_sum = state
        slot = step - behind
        active = jnp.logical_and(slot >= 0, slot < micro_count)
        group_index = jnp.clip(slot, 0, micro_count - 1)
        upstream = jnp.where(section_index == sections - 1, pick(upstreams, group_index), incoming)
        shared_upstream = lax.all_gather(upstream[0], "dp", axis=0)
        shared_joined = lax.all_gather(last_rows, "dp", axis=0)
        down_grad, grad_joined_rows, gain_part = layer_backward(
            pick(sources, group_index),
            gain_row,
            pick(joineds, group_index),
            pick(probs, group_index),
            full_joined,
            full_out,
            upstream,
        )
        all_upstream = lax.dynamic_update_index_in_dim(
            all_upstream, shared_upstream, place_of(slot), 0
        )
        all_joined = lax.dynamic_update_index_in_dim(
            all_joined, shared_joined, place_of(slot - 1), 0
        )
        gain_sum = gain_sum + jnp.where(active, gain_part, 0.0)
        incoming = from_behind(down_grad, "section", -1)
        return (incoming, grad_joined_rows[0], all_upstream, all_joined, gain_sum)

    start_back = (
        rest,
        jnp.zeros((length, joined_width), jnp.bfloat16),
        store_of(replicas, length, model_width),
        store_of(replicas, length, joined_width),
        jnp.zeros((model_width,), jnp.float32),
    )
    _, last_rows, all_upstream, all_joined, gain_sum = lax.fori_loop(
        0, step_count, backward_step, start_back
    )
    all_joined = lax.dynamic_update_index_in_dim(
        all_joined, lax.all_gather(last_rows, "dp", axis=0), place_of(step_count - 1 - behind), 0
    )
    gain_total = jnp.sum(lax.all_gather(gain_sum, "dp", axis=0), axis=0)
    valid_upstream = all_upstream[:micro_count]
    valid_joined = all_joined[:micro_count]

    def flat(rows):
        return rows.reshape(-1, rows.shape[-1])

    over_rows = (((0,), (0,)), ((), ()))
    grad_joined = lax.dot_general(
        flat(columns_normed), flat(valid_joined), over_rows, preferred_element_type=jnp.float32
    )
    grad_output = lax.dot_general(
        flat(columns_mixed), flat(valid_upstream), over_rows, preferred_element_type=jnp.float32
    )
    return (grad_joined[None], grad_output[None], gain_total[None])


def solution(mesh):
    return jax.shard_map(
        body,
        mesh=mesh,
        in_specs=(
            P(("groups", "dp"), None),
            P(("groups", "dp"), None),
            P(("groups", "dp"), None, None),
            P("section", None),
            P("section", "dp", None),
            P("section", "dp", None),
        ),
        out_specs=(
            P(("groups", "section"), "dp", None),
            P(("groups", "section"), "dp", None),
            P(("groups", "section"), None),
        ),
        check_vma=False,
    )
```

profile of v0, /device:TPU:0, one launch (start us, length us, event | category | flops | bytes accessed | tf_op | source)
XLA Modules:
  0.0 662.7 jit_solution(814957823230022412)
XLA Ops:
  9.2 67.4 %all-gather.14.cloned.1.call-done = bf16[1,1536,3072]{2,1,0:T(8,128)(2,1)} async-done(((bf16[1,384,3072]{2,1,0:T(8,128)(2,1)}), bf16[1,1536,3072]{2,1,0:T(8,128)(2,1)}) %all-gather.14.cloned.1.call-update) | async-done | bytes 9437200 | tf_op jit(solution)/shard_map/all_gather | solution.py:127
  76.5 70.3 %all-gather.12.cloned.1.call-done = bf16[1,3072,1664]{2,1,0:T(8,128)(2,1)} async-done(((bf16[1,768,1664]{2,1,0:T(8,128)(2,1)}), bf16[1,3072,1664]{2,1,0:T(8,128)(2,1)}) %all-gather.12.cloned.1.call-update) | async-done | bytes 10223632 | tf_op jit(solution)/shard_map/all_gather | solution.py:126
  152.4 185.4 %while.48 = (s32[]{:T(128)}, bf16[1,48,3072]{2,1,0:T(8,128)(2,1)}, bf16[4,1,48,3072]{3,2,1,0:T(8,128)(2,1)}, bf16[4,1,48,1664]{3,2,1,0:T(8,128)(2,1)}, f32[4,1,2...) while((s32[]{:T(128)}, bf16[1,48,3072]{2,1,0:T(8,128)(2,1)}, ...), condition=%wide.region_5.6_spmd, body=%wide.region_1.5_spmd.sunk | while | flops 960790336 | bytes 28933956 | solution.py:192
  250.1 6.5 bitcast_dynamic-update-slice_fusion.17
  280.6 6.5 bitcast_dynamic-update-slice_fusion.17
  310.8 6.5 bitcast_dynamic-update-slice_fusion.17
  348.5 270.0 %while.49 = (s32[]{:T(128)}, bf16[1,48,3072]{2,1,0:T(8,128)(2,1)}, bf16[48,1664]{1,0:T(8,128)(2,1)S(1)}, bf16[4,4,48,3072]{3,2,1,0:T(8,128)(2,1)}, bf16[4,4,48,1...) while((s32[]{:T(128)}, bf16[1,48,3072]{2,1,0:T(8,128)(2,1)}, ...), condition=%wide.region_11.12_spmd.clone, body=%wide.region_6.11_spmd.clone.sunk | while | flops 975469632 | bytes 40366604 | solution.py:236
  351.3 6.8 %convolution_convert_fusion.5 = bf16[48,1536]{1,0:T(8,128)(2,1)S(1)} fusion(bf16[1536,3072]{1,0:T(8,128)(2,1)} %get-tuple-element.1081, bf16[1,48,3072]{2,1,0:T(8,128)(2,1)} %bitcast_select_fusion.4), kind=kOutput, calls=%fused_computation.31.clone.1 | convolution fusion | flops 453058560 | bytes 9879552 | tf_op jit(solution)/shard_map/while/body/eval_jaxpr/dot_general | solution.py:80
  365.2 7.8 %all-gather.7 = bf16[192,1664]{1,0:T(8,128)(2,1)S(1)} all-gather(bf16[48,1664]{1,0:T(8,128)(2,1)S(1)} %get-tuple-element.1050), channel_id=2, replica_groups=mesh['groups'=2,'section'=4,'dp'=4] {'dp'}, dimensions={0}, use_global_device_ids=true | all-gather | bytes 798720 | tf_op jit(solution)/shard_map/while/body/eval_jaxpr/all_gather | solution.py:209
  373.1 7.2 %fusion.106 = (f32[3072]{0:T(1024)S(1)}, f32[48]{0:T(128)S(1)}, f32[48,3072]{1,0:T(8,128)S(1)}) fusion(f32[48]{0:T(128)S(1)} %get-tuple-element.966, bf16[4,1,48,3072]{3,2,1,0:T(8,128)(2,1)} %get-tuple-element.1078, s32[]{:T(128)S(6)} %min.23, f32[3072]{0:T(1024)S(1)} %bitcast.279, bf16[48,1664]{1,0:T(8,128)(2,1)S(1)} %concatenate.21, ...), kind=kOutput, calls=%fused_computation.52.clone.1 | convolution fusion | flops 491762624 | bytes 11293060 | tf_op jit(solution)/shard_map/while/body/eval_jaxpr/dot_general | solution.py:104
  387.0 7.3 %collective-permute-done.1 = bf16[1,48,3072]{2,1,0:T(8,128)(2,1)} collective-permute-done((bf16[1,48,3072]{2,1,0:T(8,128)(2,1)}, bf16[1,48,3072]{2,1,0:T(8,128)(2,1)}, u32[]{:S(2)}, u32[]{:S(2)}) %collective-permute-start.1) | collective-permute-done | bytes 294944 | tf_op jit(solution)/shard_map/while/body/eval_jaxpr/ppermute | solution.py:15
  397.1 6.8 %convolution_convert_fusion.5 = bf16[48,1536]{1,0:T(8,128)(2,1)S(1)} fusion(bf16[1536,3072]{1,0:T(8,128)(2,1)} %get-tuple-element.1081, bf16[1,48,3072]{2,1,0:T(8,128)(2,1)} %bitcast_select_fusion.4), kind=kOutput, calls=%fused_computation.31.clone.1 | convolution fusion | flops 453058560 | bytes 9879552 | tf_op jit(solution)/shard_map/while/body/eval_jaxpr/dot_general | solution.py:80
  411.0 7.3 %all-gather.7 = bf16[192,1664]{1,0:T(8,128)(2,1)S(1)} all-gather(bf16[48,1664]{1,0:T(8,128)(2,1)S(1)} %get-tuple-element.1050), channel_id=2, replica_groups=mesh['groups'=2,'section'=4,'dp'=4] {'dp'}, dimensions={0}, use_global_device_ids=true | all-gather | bytes 798720 | tf_op jit(solution)/shard_map/while/body/eval_jaxpr/all_gather | solution.py:209
  418.5 7.2 %fusion.106 = (f32[3072]{0:T(1024)S(1)}, f32[48]{0:T(128)S(1)}, f32[48,3072]{1,0:T(8,128)S(1)}) fusion(f32[48]{0:T(128)S(1)} %get-tuple-element.966, bf16[4,1,48,3072]{3,2,1,0:T(8,128)(2,1)} %get-tuple-element.1078, s32[]{:T(128)S(6)} %min.23, f32[3072]{0:T(1024)S(1)} %bitcast.279, bf16[48,1664]{1,0:T(8,128)(2,1)S(1)} %concatenate.21, ...), kind=kOutput, calls=%fused_computation.52.clone.1 | convolution fusion | flops 491762624 | bytes 11293060 | tf_op jit(solution)/shard_map/while/body/eval_jaxpr/dot_general | solution.py:104
  432.3 6.8 %collective-permute-done.1 = bf16[1,48,3072]{2,1,0:T(8,128)(2,1)} collective-permute-done((bf16[1,48,3072]{2,1,0:T(8,128)(2,1)}, bf16[1,48,3072]{2,1,0:T(8,128)(2,1)}, u32[]{:S(2)}, u32[]{:S(2)}) %collective-permute-start.1) | collective-permute-done | bytes 294944 | tf_op jit(solution)/shard_map/while/body/eval_jaxpr/ppermute | solution.py:15
  441.9 6.8 %convolution_convert_fusion.5 = bf16[48,1536]{1,0:T(8,128)(2,1)S(1)} fusion(bf16[1536,3072]{1,0:T(8,128)(2,1)} %get-tuple-element.1081, bf16[1,48,3072]{2,1,0:T(8,128)(2,1)} %bitcast_select_fusion.4), kind=kOutput, calls=%fused_computation.31.clone.1 | convolution fusion | flops 453058560 | bytes 9879552 | tf_op jit(solution)/shard_map/while/body/eval_jaxpr/dot_general | solution.py:80
  455.9 7.3 %all-gather.7 = bf16[192,1664]{1,0:T(8,128)(2,1)S(1)} all-gather(bf16[48,1664]{1,0:T(8,128)(2,1)S(1)} %get-tuple-element.1050), channel_id=2, replica_groups=mesh['groups'=2,'section'=4,'dp'=4] {'dp'}, dimensions={0}, use_global_device_ids=true | all-gather | bytes 798720 | tf_op jit(solution)/shard_map/while/body/eval_jaxpr/all_gather | solution.py:209
  463.3 7.2 %fusion.106 = (f32[3072]{0:T(1024)S(1)}, f32[48]{0:T(128)S(1)}, f32[48,3072]{1,0:T(8,128)S(1)}) fusion(f32[48]{0:T(128)S(1)} %get-tuple-element.966, bf16[4,1,48,3072]{3,2,1,0:T(8,128)(2,1)} %get-tuple-element.1078, s32[]{:T(128)S(6)} %min.23, f32[3072]{0:T(1024)S(1)} %bitcast.279, bf16[48,1664]{1,0:T(8,128)(2,1)S(1)} %concatenate.21, ...), kind=kOutput, calls=%fused_computation.52.clone.1 | convolution fusion | flops 491762624 | bytes 11293060 | tf_op jit(solution)/shard_map/while/body/eval_jaxpr/dot_general | solution.py:104
  477.1 6.8 %collective-permute-done.1 = bf16[1,48,3072]{2,1,0:T(8,128)(2,1)} collective-permute-done((bf16[1,48,3072]{2,1,0:T(8,128)(2,1)}, bf16[1,48,3072]{2,1,0:T(8,128)(2,1)}, u32[]{:S(2)}, u32[]{:S(2)}) %collective-permute-start.1) | collective-permute-done | bytes 294944 | tf_op jit(solution)/shard_map/while/body/eval_jaxpr/ppermute | solution.py:15
  486.8 6.8 %convolution_convert_fusion.5 = bf16[48,1536]{1,0:T(8,128)(2,1)S(1)} fusion(bf16[1536,3072]{1,0:T(8,128)(2,1)} %get-tuple-element.1081, bf16[1,48,3072]{2,1,0:T(8,128)(2,1)} %bitcast_select_fusion.4), kind=kOutput, calls=%fused_computation.31.clone.1 | convolution fusion | flops 453058560 | bytes 9879552 | tf_op jit(solution)/shard_map/while/body/eval_jaxpr/dot_general | solution.py:80
  500.7 7.3 %all-gather.7 = bf16[192,1664]{1,0:T(8,128)(2,1)S(1)} all-gather(bf16[48,1664]{1,0:T(8,128)(2,1)S(1)} %get-tuple-element.1050), channel_id=2, replica_groups=mesh['groups'=2,'section'=4,'dp'=4] {'dp'}, dimensions={0}, use_global_device_ids=true | all-gather | bytes 798720 | tf_op jit(solution)/shard_map/while/body/eval_jaxpr/all_gather | solution.py:209
  508.2 7.2 %fusion.106 = (f32[3072]{0:T(1024)S(1)}, f32[48]{0:T(128)S(1)}, f32[48,3072]{1,0:T(8,128)S(1)}) fusion(f32[48]{0:T(128)S(1)} %get-tuple-element.966, bf16[4,1,48,3072]{3,2,1,0:T(8,128)(2,1)} %get-tuple-element.1078, s32[]{:T(128)S(6)} %min.23, f32[3072]{0:T(1024)S(1)} %bitcast.279, bf16[48,1664]{1,0:T(8,128)(2,1)S(1)} %concatenate.21, ...), kind=kOutput, calls=%fused_computation.52.clone.1 | convolution fusion | flops 491762624 | bytes 11293060 | tf_op jit(solution)/shard_map/while/body/eval_jaxpr/dot_general | solution.py:104
  522.0 6.8 %collective-permute-done.1 = bf16[1,48,3072]{2,1,0:T(8,128)(2,1)} collective-permute-done((bf16[1,48,3072]{2,1,0:T(8,128)(2,1)}, bf16[1,48,3072]{2,1,0:T(8,128)(2,1)}, u32[]{:S(2)}, u32[]{:S(2)}) %collective-permute-start.1) | collective-permute-done | bytes 294944 | tf_op jit(solution)/shard_map/while/body/eval_jaxpr/ppermute | solution.py:15
  531.6 6.8 %convolution_convert_fusion.5 = bf16[48,1536]{1,0:T(8,128)(2,1)S(1)} fusion(bf16[1536,3072]{1,0:T(8,128)(2,1)} %get-tuple-element.1081, bf16[1,48,3072]{2,1,0:T(8,128)(2,1)} %bitcast_select_fusion.4), kind=kOutput, calls=%fused_computation.31.clone.1 | convolution fusion | flops 453058560 | bytes 9879552 | tf_op jit(solution)/shard_map/while/body/eval_jaxpr/dot_general | solution.py:80
  545.6 7.3 %all-gather.7 = bf16[192,1664]{1,0:T(8,128)(2,1)S(1)} all-gather(bf16[48,1664]{1,0:T(8,128)(2,1)S(1)} %get-tuple-element.1050), channel_id=2, replica_groups=mesh['groups'=2,'section'=4,'dp'=4] {'dp'}, dimensions={0}, use_global_device_ids=true | all-gather | bytes 798720 | tf_op jit(solution)/shard_map/while/body/eval_jaxpr/all_gather | solution.py:209
  553.0 7.2 %fusion.106 = (f32[3072]{0:T(1024)S(1)}, f32[48]{0:T(128)S(1)}, f32[48,3072]{1,0:T(8,128)S(1)}) fusion(f32[48]{0:T(128)S(1)} %get-tuple-element.966, bf16[4,1,48,3072]{3,2,1,0:T(8,128)(2,1)} %get-tuple-element.1078, s32[]{:T(128)S(6)} %min.23, f32[3072]{0:T(1024)S(1)} %bitcast.279, bf16[48,1664]{1,0:T(8,128)(2,1)S(1)} %concatenate.21, ...), kind=kOutput, calls=%fused_computation.52.clone.1 | convolution fusion | flops 491762624 | bytes 11293060 | tf_op jit(solution)/shard_map/while/body/eval_jaxpr/dot_general | solution.py:104
  566.8 6.9 %collective-permute-done.1 = bf16[1,48,3072]{2,1,0:T(8,128)(2,1)} collective-permute-done((bf16[1,48,3072]{2,1,0:T(8,128)(2,1)}, bf16[1,48,3072]{2,1,0:T(8,128)(2,1)}, u32[]{:S(2)}, u32[]{:S(2)}) %collective-permute-start.1) | collective-permute-done | bytes 294944 | tf_op jit(solution)/shard_map/while/body/eval_jaxpr/ppermute | solution.py:15
  576.5 6.8 %convolution_convert_fusion.5 = bf16[48,1536]{1,0:T(8,128)(2,1)S(1)} fusion(bf16[1536,3072]{1,0:T(8,128)(2,1)} %get-tuple-element.1081, bf16[1,48,3072]{2,1,0:T(8,128)(2,1)} %bitcast_select_fusion.4), kind=kOutput, calls=%fused_computation.31.clone.1 | convolution fusion | flops 453058560 | bytes 9879552 | tf_op jit(solution)/shard_map/while/body/eval_jaxpr/dot_general | solution.py:80
  590.4 7.3 %all-gather.7 = bf16[192,1664]{1,0:T(8,128)(2,1)S(1)} all-gather(bf16[48,1664]{1,0:T(8,128)(2,1)S(1)} %get-tuple-element.1050), channel_id=2, replica_groups=mesh['groups'=2,'section'=4,'dp'=4] {'dp'}, dimensions={0}, use_global_device_ids=true | all-gather | bytes 798720 | tf_op jit(solution)/shard_map/while/body/eval_jaxpr/all_gather | solution.py:209
  597.9 7.2 %fusion.106 = (f32[3072]{0:T(1024)S(1)}, f32[48]{0:T(128)S(1)}, f32[48,3072]{1,0:T(8,128)S(1)}) fusion(f32[48]{0:T(128)S(1)} %get-tuple-element.966, bf16[4,1,48,3072]{3,2,1,0:T(8,128)(2,1)} %get-tuple-element.1078, s32[]{:T(128)S(6)} %min.23, f32[3072]{0:T(1024)S(1)} %bitcast.279, bf16[48,1664]{1,0:T(8,128)(2,1)S(1)} %concatenate.21, ...), kind=kOutput, calls=%fused_computation.52.clone.1 | convolution fusion | flops 491762624 | bytes 11293060 | tf_op jit(solution)/shard_map/while/body/eval_jaxpr/dot_general | solution.py:104
  611.7 6.8 %collective-permute-done.1 = bf16[1,48,3072]{2,1,0:T(8,128)(2,1)} collective-permute-done((bf16[1,48,3072]{2,1,0:T(8,128)(2,1)}, bf16[1,48,3072]{2,1,0:T(8,128)(2,1)}, u32[]{:S(2)}, u32[]{:S(2)}) %collective-permute-start.1) | collective-permute-done | bytes 294944 | tf_op jit(solution)/shard_map/while/body/eval_jaxpr/ppermute | solution.py:15
  618.5 8.6 %all-gather.3 = bf16[192,1664]{1,0:T(8,128)(2,1)S(1)} all-gather(bf16[48,1664]{1,0:T(8,128)(2,1)S(1)} %get-tuple-element.640), channel_id=5, replica_groups=mesh['groups'=2,'section'=4,'dp'=4] {'dp'}, dimensions={0}, use_global_device_ids=true | all-gather | bytes 798720 | tf_op jit(solution)/shard_map/all_gather | solution.py:240
  (451 shorter events, 310.9 us)
Async XLA Ops:
  7.2 69.4 %all-gather.14.cloned.1.call-start = ((), (), s32[]{:S(2)}) async-start(), calls=%async_computation.1 | async-start | bytes 11796480 | tf_op jit(solution)/shard_map/all_gather | solution.py:127
  7.9 138.9 %all-gather.12.cloned.1.call-start = ((), (), s32[]{:S(2)}) async-start(), calls=%async_computation | async-start | bytes 12779520 | tf_op jit(solution)/shard_map/all_gather | solution.py:126
  173.6 10.5 %collective-permute-start = (bf16[1,48,3072]{2,1,0:T(8,128)(2,1)}, bf16[1,48,3072]{2,1,0:T(8,128)(2,1)}, u32[]{:S(2)}, u32[]{:S(2)}) collective-permute-start(bf16[1,48,3072]{2,1,0:T(8,128)(2,1)} %fusion.90), channel_id=1, source_target_pairs={{0,4},{4,8},{8,12},{1,5},{5,9},{9,13},{2,6},{6,10},{10,14},{3,7},{... | collective-permute-start | bytes 884744 | tf_op jit(solution)/shard_map/while/body/eval_jaxpr/ppermute | solution.py:15
  205.3 10.6 %collective-permute-start = (bf16[1,48,3072]{2,1,0:T(8,128)(2,1)}, bf16[1,48,3072]{2,1,0:T(8,128)(2,1)}, u32[]{:S(2)}, u32[]{:S(2)}) collective-permute-start(bf16[1,48,3072]{2,1,0:T(8,128)(2,1)} %fusion.90), channel_id=1, source_target_pairs={{0,4},{4,8},{8,12},{1,5},{5,9},{9,13},{2,6},{6,10},{10,14},{3,7},{... | collective-permute-start | bytes 884744 | tf_op jit(solution)/shard_map/while/body/eval_jaxpr/ppermute | solution.py:15
  237.1 9.7 %collective-permute-start = (bf16[1,48,3072]{2,1,0:T(8,128)(2,1)}, bf16[1,48,3072]{2,1,0:T(8,128)(2,1)}, u32[]{:S(2)}, u32[]{:S(2)}) collective-permute-start(bf16[1,48,3072]{2,1,0:T(8,128)(2,1)} %fusion.90), channel_id=1, source_target_pairs={{0,4},{4,8},{8,12},{1,5},{5,9},{9,13},{2,6},{6,10},{10,14},{3,7},{... | collective-permute-start | bytes 884744 | tf_op jit(solution)/shard_map/while/body/eval_jaxpr/ppermute | solution.py:15
  268.1 9.3 %collective-permute-start = (bf16[1,48,3072]{2,1,0:T(8,128)(2,1)}, bf16[1,48,3072]{2,1,0:T(8,128)(2,1)}, u32[]{:S(2)}, u32[]{:S(2)}) collective-permute-start(bf16[1,48,3072]{2,1,0:T(8,128)(2,1)} %fusion.90), channel_id=1, source_target_pairs={{0,4},{4,8},{8,12},{1,5},{5,9},{9,13},{2,6},{6,10},{10,14},{3,7},{... | collective-permute-start | bytes 884744 | tf_op jit(solution)/shard_map/while/body/eval_jaxpr/ppermute | solution.py:15
  298.6 9.0 %collective-permute-start = (bf16[1,48,3072]{2,1,0:T(8,128)(2,1)}, bf16[1,48,3072]{2,1,0:T(8,128)(2,1)}, u32[]{:S(2)}, u32[]{:S(2)}) collective-permute-start(bf16[1,48,3072]{2,1,0:T(8,128)(2,1)} %fusion.90), channel_id=1, source_target_pairs={{0,4},{4,8},{8,12},{1,5},{5,9},{9,13},{2,6},{6,10},{10,14},{3,7},{... | collective-permute-start | bytes 884744 | tf_op jit(solution)/shard_map/while/body/eval_jaxpr/ppermute | solution.py:15
  328.8 9.0 %collective-permute-start = (bf16[1,48,3072]{2,1,0:T(8,128)(2,1)}, bf16[1,48,3072]{2,1,0:T(8,128)(2,1)}, u32[]{:S(2)}, u32[]{:S(2)}) collective-permute-start(bf16[1,48,3072]{2,1,0:T(8,128)(2,1)} %fusion.90), channel_id=1, source_target_pairs={{0,4},{4,8},{8,12},{1,5},{5,9},{9,13},{2,6},{6,10},{10,14},{3,7},{... | collective-permute-start | bytes 884744 | tf_op jit(solution)/shard_map/while/body/eval_jaxpr/ppermute | solution.py:15
  340.1 310.2 %collective-permute-start.4 = (bf16[3,48,768]{2,1,0:T(8,128)(2,1)}, bf16[3,48,768]{2,1,0:T(8,128)(2,1)}, u32[]{:S(2)}, u32[]{:S(2)}) collective-permute-start(bf16[3,48,768]{2,1,0:T(8,128)(2,1)} %get-tuple-element.763), channel_id=1, source_target_pairs={{0,3},{1,0},{2,1},{3,2},{4,7},{5,4},{6,5},{7,6},{8,11},{9,8},{10,9... | collective-permute-start | bytes 663560 | tf_op jit(solution)/shard_map/ppermute | solution.py:141
  340.1 309.2 %collective-permute-start.3 = (bf16[3,48,768]{2,1,0:T(8,128)(2,1)}, bf16[3,48,768]{2,1,0:T(8,128)(2,1)}, u32[]{:S(2)}, u32[]{:S(2)}) collective-permute-start(bf16[3,48,768]{2,1,0:T(8,128)(2,1)} %get-tuple-element.764), channel_id=1, source_target_pairs={{0,2},{1,3},{2,0},{3,1},{4,6},{5,7},{6,4},{7,5},{8,10},{9,11},{10,... | collective-permute-start | bytes 663560 | tf_op jit(solution)/shard_map/ppermute | solution.py:141
  340.6 307.7 %collective-permute-start.2 = (bf16[3,48,768]{2,1,0:T(8,128)(2,1)}, bf16[3,48,768]{2,1,0:T(8,128)(2,1)}, u32[]{:S(2)}, u32[]{:S(2)}) collective-permute-start(bf16[3,48,768]{2,1,0:T(8,128)(2,1)} %get-tuple-element.765), channel_id=1, source_target_pairs={{0,1},{1,2},{2,3},{3,0},{4,5},{5,6},{6,7},{7,4},{8,9},{9,10},{10,1... | collective-permute-start | bytes 663560 | tf_op jit(solution)/shard_map/ppermute | solution.py:141
  341.7 298.5 %collective-permute-start.7 = (bf16[3,48,384]{2,1,0:T(8,128)(2,1)}, bf16[3,48,384]{2,1,0:T(8,128)(2,1)}, u32[]{:S(2)}, u32[]{:S(2)}) collective-permute-start(bf16[3,48,384]{2,1,0:T(8,128)(2,1)} %get-tuple-element.767), channel_id=1, source_target_pairs={{0,3},{1,0},{2,1},{3,2},{4,7},{5,4},{6,5},{7,6},{8,11},{9,8},{10,9... | collective-permute-start | bytes 331784 | tf_op jit(solution)/shard_map/ppermute | solution.py:141
  348.5 36.1 %all-gather.16.cloned.1.call-start = ((), (), s32[]{:S(2)}) async-start(), calls=%async_computation.2 | async-start | bytes 1474560 | tf_op jit(solution)/shard_map/while/body/eval_jaxpr/all_gather | solution.py:208
  373.1 10.5 %copy-start.13 = (f32[3072]{0:T(1024)S(1)}, f32[3072]{0:T(1024)}, u32[]{:S(2)}) copy-start(f32[3072]{0:T(1024)} %get-tuple-element.1053) | copy-start | bytes 36868 | tf_op jit(solution)/shard_map/while
  382.3 11.9 %collective-permute-start.1 = (bf16[1,48,3072]{2,1,0:T(8,128)(2,1)}, bf16[1,48,3072]{2,1,0:T(8,128)(2,1)}, u32[]{:S(2)}, u32[]{:S(2)}) collective-permute-start(bf16[1,48,3072]{2,1,0:T(8,128)(2,1)} %fusion.107), channel_id=1, source_target_pairs={{4,0},{8,4},{12,8},{5,1},{9,5},{13,9},{6,2},{10,6},{14,10},{7,3},{... | collective-permute-start | bytes 884744 | tf_op jit(solution)/shard_map/while/body/eval_jaxpr/ppermute | solution.py:15
  383.7 10.6 %copy-start.14 = (f32[3072]{0:T(1024)}, f32[3072]{0:T(1024)S(1)}, u32[]{:S(2)}) copy-start(f32[3072]{0:T(1024)S(1)} %select_add_fusion.2) | copy-start | bytes 36868 | tf_op jit(solution)/shard_map/while
  394.2 35.7 %all-gather.16.cloned.1.call-start = ((), (), s32[]{:S(2)}) async-start(), calls=%async_computation.2 | async-start | bytes 1474560 | tf_op jit(solution)/shard_map/while/body/eval_jaxpr/all_gather | solution.py:208
  418.4 10.5 %copy-start.13 = (f32[3072]{0:T(1024)S(1)}, f32[3072]{0:T(1024)}, u32[]{:S(2)}) copy-start(f32[3072]{0:T(1024)} %get-tuple-element.1053) | copy-start | bytes 36868 | tf_op jit(solution)/shard_map/while
  427.6 11.5 %collective-permute-start.1 = (bf16[1,48,3072]{2,1,0:T(8,128)(2,1)}, bf16[1,48,3072]{2,1,0:T(8,128)(2,1)}, u32[]{:S(2)}, u32[]{:S(2)}) collective-permute-start(bf16[1,48,3072]{2,1,0:T(8,128)(2,1)} %fusion.107), channel_id=1, source_target_pairs={{4,0},{8,4},{12,8},{5,1},{9,5},{13,9},{6,2},{10,6},{14,10},{7,3},{... | collective-permute-start | bytes 884744 | tf_op jit(solution)/shard_map/while/body/eval_jaxpr/ppermute | solution.py:15
  439.1 35.6 %all-gather.16.cloned.1.call-start = ((), (), s32[]{:S(2)}) async-start(), calls=%async_computation.2 | async-start | bytes 1474560 | tf_op jit(solution)/shard_map/while/body/eval_jaxpr/all_gather | solution.py:208
  463.3 10.5 %copy-start.13 = (f32[3072]{0:T(1024)S(1)}, f32[3072]{0:T(1024)}, u32[]{:S(2)}) copy-start(f32[3072]{0:T(1024)} %get-tuple-element.1053) | copy-start | bytes 36868 | tf_op jit(solution)/shard_map/while
  472.5 11.5 %collective-permute-start.1 = (bf16[1,48,3072]{2,1,0:T(8,128)(2,1)}, bf16[1,48,3072]{2,1,0:T(8,128)(2,1)}, u32[]{:S(2)}, u32[]{:S(2)}) collective-permute-start(bf16[1,48,3072]{2,1,0:T(8,128)(2,1)} %fusion.107), channel_id=1, source_target_pairs={{4,0},{8,4},{12,8},{5,1},{9,5},{13,9},{6,2},{10,6},{14,10},{7,3},{... | collective-permute-start | bytes 884744 | tf_op jit(solution)/shard_map/while/body/eval_jaxpr/ppermute | solution.py:15
  483.9 35.7 %all-gather.16.cloned.1.call-start = ((), (), s32[]{:S(2)}) async-start(), calls=%async_computation.2 | async-start | bytes 1474560 | tf_op jit(solution)/shard_map/while/body/eval_jaxpr/all_gather | solution.py:208
  508.2 10.5 %copy-start.13 = (f32[3072]{0:T(1024)S(1)}, f32[3072]{0:T(1024)}, u32[]{:S(2)}) copy-start(f32[3072]{0:T(1024)} %get-tuple-element.1053) | copy-start | bytes 36868 | tf_op jit(solution)/shard_map/while
  517.3 11.5 %collective-permute-start.1 = (bf16[1,48,3072]{2,1,0:T(8,128)(2,1)}, bf16[1,48,3072]{2,1,0:T(8,128)(2,1)}, u32[]{:S(2)}, u32[]{:S(2)}) collective-permute-start(bf16[1,48,3072]{2,1,0:T(8,128)(2,1)} %fusion.107), channel_id=1, source_target_pairs={{4,0},{8,4},{12,8},{5,1},{9,5},{13,9},{6,2},{10,6},{14,10},{7,3},{... | collective-permute-start | bytes 884744 | tf_op jit(solution)/shard_map/while/body/eval_jaxpr/ppermute | solution.py:15
  528.8 35.6 %all-gather.16.cloned.1.call-start = ((), (), s32[]{:S(2)}) async-start(), calls=%async_computation.2 | async-start | bytes 1474560 | tf_op jit(solution)/shard_map/while/body/eval_jaxpr/all_gather | solution.py:208
  562.2 11.5 %collective-permute-start.1 = (bf16[1,48,3072]{2,1,0:T(8,128)(2,1)}, bf16[1,48,3072]{2,1,0:T(8,128)(2,1)}, u32[]{:S(2)}, u32[]{:S(2)}) collective-permute-start(bf16[1,48,3072]{2,1,0:T(8,128)(2,1)} %fusion.107), channel_id=1, source_target_pairs={{4,0},{8,4},{12,8},{5,1},{9,5},{13,9},{6,2},{10,6},{14,10},{7,3},{... | collective-permute-start | bytes 884744 | tf_op jit(solution)/shard_map/while/body/eval_jaxpr/ppermute | solution.py:15
  573.6 35.7 %all-gather.16.cloned.1.call-start = ((), (), s32[]{:S(2)}) async-start(), calls=%async_computation.2 | async-start | bytes 1474560 | tf_op jit(solution)/shard_map/while/body/eval_jaxpr/all_gather | solution.py:208
  597.8 10.5 %copy-start.13 = (f32[3072]{0:T(1024)S(1)}, f32[3072]{0:T(1024)}, u32[]{:S(2)}) copy-start(f32[3072]{0:T(1024)} %get-tuple-element.1053) | copy-start | bytes 36868 | tf_op jit(solution)/shard_map/while
  607.0 11.5 %collective-permute-start.1 = (bf16[1,48,3072]{2,1,0:T(8,128)(2,1)}, bf16[1,48,3072]{2,1,0:T(8,128)(2,1)}, u32[]{:S(2)}, u32[]{:S(2)}) collective-permute-start(bf16[1,48,3072]{2,1,0:T(8,128)(2,1)} %fusion.107), channel_id=1, source_target_pairs={{4,0},{8,4},{12,8},{5,1},{9,5},{13,9},{6,2},{10,6},{14,10},{7,3},{... | collective-permute-start | bytes 884744 | tf_op jit(solution)/shard_map/while/body/eval_jaxpr/ppermute | solution.py:15
  618.5 15.6 %collective-permute-start.5 = (bf16[3,48,384]{2,1,0:T(8,128)(2,1)}, bf16[3,48,384]{2,1,0:T(8,128)(2,1)S(1)}, u32[]{:S(2)}, u32[]{:S(2)}) collective-permute-start(bf16[3,48,384]{2,1,0:T(8,128)(2,1)} %get-tuple-element.769), channel_id=1, source_target_pairs={{0,1},{1,2},{2,3},{3,0},{4,5},{5,6},{6,7},{7,4},{8,9},{9,10},{10,1... | collective-permute-start | bytes 331784 | tf_op jit(solution)/shard_map/ppermute | solution.py:141
  634.1 5.5 collective-permute-start.6
  (67 other events, 363.4 us)
Sparse Core Ops, SparseCore 0:
  9.6 66.9 all-gather.13
  78.1 68.6 all-gather.11
  350.9 19.0 all-gather.15
  396.3 16.7 all-gather.15
  441.2 17.1 all-gather.15
  486.0 17.0 all-gather.15
  531.2 17.2 all-gather.15
  576.0 17.0 all-gather.15
where the time goes:
time: 667 us; the launch traced here: 663 us
  matrix products  208 us (31%)
  waiting for transfers between devices  188 us (28%)
  local copies, waits for them, and re-layouts  90.4 us (14%)
  other arithmetic  60.8 us (9%)
  blocking collectives  58.4 us (9%)
  starting transfers between devices  40.5 us (6%)
  between operations  14.3 us (2%)
    all_gather x1, waiting for transfers between devices, gather_weights(): lax.all_gather(w_joined[0], 'dp', axis=0, tiled=True)  70.3 us
    all_gather x1, waiting for transfers between devices, gather_weights(): lax.all_gather(w_out[0], 'dp', axis=0, tiled=True)  67.4 us
    ppermute x12, waiting for transfers between devices, from_behind(): lax.ppermute(value, axis, [(source, source + steps) for source in range(i...  45.4 us
    all_gather x6, blocking collectives, backward_step(): shared_joined = lax.all_gather(last_rows, 'dp', axis=0)  44.4 us
    dot_general x6, matrix products, layer_backward(): lax.dot_general(grad_joined_rows.reshape(-1, grad_joined_rows.shape[2]),...  43.3 us
    dot_general x6, matrix products, layer_backward(): lax.dot_general(upstream.reshape(-1, model_width), w_out, (((1,), (1,)),...  40.7 us
    dot_general x6, matrix products, project(): jnp.dot(normed.reshape(-1, model_width), weight, preferred_element_type=j...  39.1 us
    dot_general x6, matrix products, layer_forward(): jnp.dot(mixed_heads.reshape(-1, mixed_heads.shape[2]), w_out, preferred_e...  37.3 us
  transfers between devices with their start and end apart: 26, of which 12 were waited for; matrix products, arithmetic and copies ran while one was open for 33% of the time, Pallas kernels for 0%

commit v1 on v0

--- a/solution.py
+++ b/solution.py
@@ -7,6 +7,28 @@
 HEAD_DIM = 64
 BLOCK_LEN = 16
 EPSILON = 1e-05
+
+
+def laid_out(parts, dim):
+    parts = jnp.moveaxis(parts, 0, dim)
+    lengths = parts.shape
+    return parts.reshape(*lengths[:dim], lengths[dim] * lengths[dim + 1], *lengths[dim + 2 :])
+
+
+def gather_around(shard, axis, dim):
+    peers = lax.axis_size(axis)
+    pairs = [(i, (i + 1) % peers) for i in range(peers)]
+    back = [(b, a) for a, b in pairs]
+    lower, upper = ([], [])
+    for step in range(peers - 1):
+        if step % 2 == 0:
+            lower.append(lax.ppermute(lower[-1] if lower else shard, axis, pairs))
+        else:
+            upper.append(lax.ppermute(upper[-1] if upper else shard, axis, back))
+    parts = jnp.stack([*lower[::-1], shard, *upper])
+    shift = lax.axis_index(axis) - len(lower)
+    parts = parts[(jnp.arange(peers) - shift) % peers]
+    return laid_out(parts, dim)
 
 
 def from_behind(value, axis, steps):
@@ -122,10 +144,7 @@
 
 
 def gather_weights(w_joined, w_out):
-    return (
-        lax.all_gather(w_joined[0], "dp", axis=0, tiled=True),
-        lax.all_gather(w_out[0], "dp", axis=0, tiled=True),
-    )
+    return (gather_around(w_joined[0], "dp", 0), lax.all_gather(w_out[0], "dp", axis=0, tiled=True))
 
 
 def share_columns(rows):

time: 667 us -> 690 us (1.034)
  local copies, waits for them, and re-layouts: 90.4 us -> 109 us
  waiting for transfers between devices: 188 us -> 170 us
  blocking collectives: 58.4 us -> 76 us
  matrix products: 208 us -> 192 us
  starting transfers between devices: 40.5 us -> 51.6 us
  other arithmetic: 60.8 us -> 71.3 us
    ppermute x0 -> x3, waiting for transfers between devices: none -> 126 us  [the longest x2 126 us: gather_around(): lower.append(lax.ppermute(lower[-1] if lower else shard, axis, pairs))]
    all_gather x1 -> x0, waiting for transfers between devices: 70.3 us -> none  [gather_weights(): lax.all_gather(w_joined[0], 'dp', axis=0, tiled=True)]
    all_gather x1, waiting for transfers between devices: 67.4 us -> 0.01 us  [gather_weights(): lax.all_gather(w_out[0], 'dp', axis=0, tiled=True)]
    all_gather x6, blocking collectives: 44.4 us -> 63.7 us  [backward_step(): shared_joined = lax.all_gather(last_rows, 'dp', axis=0)]
    gather x0 -> x3, local copies, waits for them, and re-layouts: none -> 14.4 us  [gather_around(): parts = parts[(jnp.arange(peers) - shift) % peers]]
    ppermute x0 -> x3, starting transfers between devices: none -> 9.68 us  [the longest x2 7.69 us: gather_around(): lower.append(lax.ppermute(lower[-1] if lower else shard, axis, pairs))]
    unnamed x1 -> x2, other arithmetic: 0.01 us -> 9.39 us
    dot_general x6, matrix products: 10.7 us -> 2.85 us  [layer_backward(): jnp.einsum('bihd,bjd->bhij', grad_mixed, values, preferred_element_type=j...]
  transfers between devices with their start and end apart: 26 -> 28, of which waited for: 12 -> 10; matrix products, arithmetic and copies ran while one was open for 33% -> 34% of each run, Pallas kernels for 0% -> 0%
where the time goes in v1:
time: 690 us; the launch traced here: 685 us
  matrix products  192 us (28%)
  waiting for transfers between devices  170 us (25%)
  local copies, waits for them, and re-layouts  109 us (16%)
  blocking collectives  76 us (11%)
  other arithmetic  71.3 us (10%)
  starting transfers between devices  51.6 us (7%)
  between operations  14.2 us (2%)
    ppermute x2, waiting for transfers between devices, gather_around(): lower.append(lax.ppermute(lower[-1] if lower else shard, axis, pairs))  126 us
    all_gather x6, blocking collectives, backward_step(): shared_joined = lax.all_gather(last_rows, 'dp', axis=0)  63.7 us
    dot_general x6, matrix products, layer_backward(): lax.dot_general(grad_joined_rows.reshape(-1, grad_joined_rows.shape[2]),...  43.3 us
    ppermute x12, waiting for transfers between devices, from_behind(): lax.ppermute(value, axis, [(source, source + steps) for source in range(i...  41.3 us
    dot_general x6, matrix products, layer_backward(): lax.dot_general(upstream.reshape(-1, model_width), w_out, (((1,), (1,)),...  40.4 us
    dot_general x6, matrix products, project(): jnp.dot(normed.reshape(-1, model_width), weight, preferred_element_type=j...  39 us
    ppermute x12, starting transfers between devices, from_behind(): lax.ppermute(value, axis, [(source, source + steps) for source in range(i...  37.6 us
    dot_general x6, matrix products, layer_forward(): jnp.dot(mixed_heads.reshape(-1, mixed_heads.shape[2]), w_out, preferred_e...  37.4 us
  transfers between devices with their start and end apart: 28, of which 10 were waited for; matrix products, arithmetic and copies ran while one was open for 34% of the time, Pallas kernels for 0%

profile of v1, /device:TPU:0, one launch (start us, length us, event | category | flops | bytes accessed | tf_op | source)
XLA Modules:
  0.0 685.2 jit_solution(4823511099581338566)
XLA Ops:
  10.4 93.1 %collective-permute-done.2 = bf16[768,1664]{1,0:T(8,128)(2,1)S(1)} collective-permute-done((bf16[768,1664]{1,0:T(8,128)(2,1)}, bf16[768,1664]{1,0:T(8,128)(2,1)S(1)}, u32[]{:S(2)}, u32[]{:S(2)}) %collective-permute-start.2) | collective-permute-done | bytes 2555936 | tf_op jit(solution)/shard_map/ppermute | solution.py:25
  103.5 7.2 %collective-permute-start.3 = (bf16[768,1664]{1,0:T(8,128)(2,1)S(1)}, bf16[768,1664]{1,0:T(8,128)(2,1)}, u32[]{:S(2)}, u32[]{:S(2)}) collective-permute-start(bf16[768,1664]{1,0:T(8,128)(2,1)S(1)} %collective-permute-done.2), channel_id=1, source_target_pairs={{0,1},{1,2},{2,3},{3,0},{4,5},{5,6},{6,7},{7,4},{8,9},{9,10},{10,1... | collective-permute-start | bytes 7667720 | tf_op jit(solution)/shard_map/ppermute | solution.py:25
  111.9 32.8 %collective-permute-done.3 = bf16[768,1664]{1,0:T(8,128)(2,1)} collective-permute-done((bf16[768,1664]{1,0:T(8,128)(2,1)S(1)}, bf16[768,1664]{1,0:T(8,128)(2,1)}, u32[]{:S(2)}, u32[]{:S(2)}) %collective-permute-start.3) | collective-permute-done | bytes 2555936 | tf_op jit(solution)/shard_map/ppermute | solution.py:25
  168.1 9.4 %pad_maximum_fusion.1 = bf16[4,768,1664]{2,1,0:T(8,128)(2,1)} fusion(bf16[4,768,768]{2,1,0:T(8,128)(2,1)} %gather_fusion.1, bf16[4,768,896]{2,1,0:T(8,128)(2,1)} %gather_fusion), kind=kLoop, calls=%fused_computation.79 | loop fusion | flops 20447232 | bytes 20447232
  183.1 179.4 %while.48 = (s32[]{:T(128)}, bf16[1,48,3072]{2,1,0:T(8,128)(2,1)}, bf16[4,1,48,3072]{3,2,1,0:T(8,128)(2,1)}, bf16[4,1,48,1664]{3,2,1,0:T(8,128)(2,1)}, f32[4,1,2...) while((s32[]{:T(128)}, bf16[1,48,3072]{2,1,0:T(8,128)(2,1)}, ...), condition=%wide.region_5.6_spmd, body=%wide.region_1.5_spmd.sunk | while | flops 960790336 | bytes 28930116 | solution.py:211
  215.8 6.5 bitcast_dynamic-update-slice_fusion.17
  371.8 272.7 %while.49 = (s32[]{:T(128)}, bf16[1,48,3072]{2,1,0:T(8,128)(2,1)}, bf16[48,1664]{1,0:T(8,128)(2,1)S(1)}, bf16[4,4,48,3072]{3,2,1,0:T(8,128)(2,1)}, bf16[4,4,48,1...) while((s32[]{:T(128)}, bf16[1,48,3072]{2,1,0:T(8,128)(2,1)}, ...), condition=%wide.region_11.12_spmd.clone, body=%wide.region_6.11_spmd.clone.sunk | while | flops 975469632 | bytes 47283840 | solution.py:255
  374.1 6.7 convolution_convert_fusion.5
  383.4 11.6 %all-gather.6 = bf16[192,1664]{1,0:T(8,128)(2,1)S(1)} all-gather(bf16[48,1664]{1,0:T(8,128)(2,1)S(1)} %get-tuple-element.1050), channel_id=2, replica_groups=mesh['groups'=2,'section'=4,'dp'=4] {'dp'}, dimensions={0}, use_global_device_ids=true | all-gather | bytes 798720 | tf_op jit(solution)/shard_map/while/body/eval_jaxpr/all_gather | solution.py:228
  398.3 7.2 %fusion.108 = (f32[3072]{0:T(1024)S(1)}, f32[48]{0:T(128)S(1)}, f32[48,3072]{1,0:T(8,128)S(1)}) fusion(f32[48]{0:T(128)S(1)} %get-tuple-element.966, bf16[4,1,48,3072]{3,2,1,0:T(8,128)(2,1)} %get-tuple-element.1078, s32[]{:T(128)S(6)} %min.23, f32[3072]{0:T(1024)S(1)} %bitcast.289, bf16[48,1664]{1,0:T(8,128)(2,1)S(1)} %concatenate.21, ...), kind=kOutput, calls=%fused_computation.54.clone.1 | convolution fusion | flops 491762624 | bytes 11293060 | tf_op jit(solution)/shard_map/while/body/eval_jaxpr/dot_general | solution.py:126
  411.5 7.2 %collective-permute-done.1 = bf16[1,48,3072]{2,1,0:T(8,128)(2,1)} collective-permute-done((bf16[1,48,3072]{2,1,0:T(8,128)(2,1)S(1)}, bf16[1,48,3072]{2,1,0:T(8,128)(2,1)}, u32[]{:S(2)}, u32[]{:S(2)}) %collective-permute-start.1) | collective-permute-done | bytes 294944 | tf_op jit(solution)/shard_map/while/body/eval_jaxpr/ppermute | solution.py:37
  421.0 6.7 convolution_convert_fusion.5
  430.2 11.2 %all-gather.6 = bf16[192,1664]{1,0:T(8,128)(2,1)S(1)} all-gather(bf16[48,1664]{1,0:T(8,128)(2,1)S(1)} %get-tuple-element.1050), channel_id=2, replica_groups=mesh['groups'=2,'section'=4,'dp'=4] {'dp'}, dimensions={0}, use_global_device_ids=true | all-gather | bytes 798720 | tf_op jit(solution)/shard_map/while/body/eval_jaxpr/all_gather | solution.py:228
  444.8 7.2 %fusion.108 = (f32[3072]{0:T(1024)S(1)}, f32[48]{0:T(128)S(1)}, f32[48,3072]{1,0:T(8,128)S(1)}) fusion(f32[48]{0:T(128)S(1)} %get-tuple-element.966, bf16[4,1,48,3072]{3,2,1,0:T(8,128)(2,1)} %get-tuple-element.1078, s32[]{:T(128)S(6)} %min.23, f32[3072]{0:T(1024)S(1)} %bitcast.289, bf16[48,1664]{1,0:T(8,128)(2,1)S(1)} %concatenate.21, ...), kind=kOutput, calls=%fused_computation.54.clone.1 | convolution fusion | flops 491762624 | bytes 11293060 | tf_op jit(solution)/shard_map/while/body/eval_jaxpr/dot_general | solution.py:126
  458.0 6.6 collective-permute-done.1
  466.9 6.7 convolution_convert_fusion.5
  476.2 10.2 %all-gather.6 = bf16[192,1664]{1,0:T(8,128)(2,1)S(1)} all-gather(bf16[48,1664]{1,0:T(8,128)(2,1)S(1)} %get-tuple-element.1050), channel_id=2, replica_groups=mesh['groups'=2,'section'=4,'dp'=4] {'dp'}, dimensions={0}, use_global_device_ids=true | all-gather | bytes 798720 | tf_op jit(solution)/shard_map/while/body/eval_jaxpr/all_gather | solution.py:228
  489.8 7.2 %fusion.108 = (f32[3072]{0:T(1024)S(1)}, f32[48]{0:T(128)S(1)}, f32[48,3072]{1,0:T(8,128)S(1)}) fusion(f32[48]{0:T(128)S(1)} %get-tuple-element.966, bf16[4,1,48,3072]{3,2,1,0:T(8,128)(2,1)} %get-tuple-element.1078, s32[]{:T(128)S(6)} %min.23, f32[3072]{0:T(1024)S(1)} %bitcast.289, bf16[48,1664]{1,0:T(8,128)(2,1)S(1)} %concatenate.21, ...), kind=kOutput, calls=%fused_computation.54.clone.1 | convolution fusion | flops 491762624 | bytes 11293060 | tf_op jit(solution)/shard_map/while/body/eval_jaxpr/dot_general | solution.py:126
  503.0 6.6 collective-permute-done.1
  511.9 6.7 convolution_convert_fusion.5
  521.2 10.2 %all-gather.6 = bf16[192,1664]{1,0:T(8,128)(2,1)S(1)} all-gather(bf16[48,1664]{1,0:T(8,128)(2,1)S(1)} %get-tuple-element.1050), channel_id=2, replica_groups=mesh['groups'=2,'section'=4,'dp'=4] {'dp'}, dimensions={0}, use_global_device_ids=true | all-gather | bytes 798720 | tf_op jit(solution)/shard_map/while/body/eval_jaxpr/all_gather | solution.py:228
  534.7 7.2 %fusion.108 = (f32[3072]{0:T(1024)S(1)}, f32[48]{0:T(128)S(1)}, f32[48,3072]{1,0:T(8,128)S(1)}) fusion(f32[48]{0:T(128)S(1)} %get-tuple-element.966, bf16[4,1,48,3072]{3,2,1,0:T(8,128)(2,1)} %get-tuple-element.1078, s32[]{:T(128)S(6)} %min.23, f32[3072]{0:T(1024)S(1)} %bitcast.289, bf16[48,1664]{1,0:T(8,128)(2,1)S(1)} %concatenate.21, ...), kind=kOutput, calls=%fused_computation.54.clone.1 | convolution fusion | flops 491762624 | bytes 11293060 | tf_op jit(solution)/shard_map/while/body/eval_jaxpr/dot_general | solution.py:126
  547.9 6.6 collective-permute-done.1
  556.8 6.7 convolution_convert_fusion.5
  566.1 10.2 %all-gather.6 = bf16[192,1664]{1,0:T(8,128)(2,1)S(1)} all-gather(bf16[48,1664]{1,0:T(8,128)(2,1)S(1)} %get-tuple-element.1050), channel_id=2, replica_groups=mesh['groups'=2,'section'=4,'dp'=4] {'dp'}, dimensions={0}, use_global_device_ids=true | all-gather | bytes 798720 | tf_op jit(solution)/shard_map/while/body/eval_jaxpr/all_gather | solution.py:228
  579.7 7.2 %fusion.108 = (f32[3072]{0:T(1024)S(1)}, f32[48]{0:T(128)S(1)}, f32[48,3072]{1,0:T(8,128)S(1)}) fusion(f32[48]{0:T(128)S(1)} %get-tuple-element.966, bf16[4,1,48,3072]{3,2,1,0:T(8,128)(2,1)} %get-tuple-element.1078, s32[]{:T(128)S(6)} %min.23, f32[3072]{0:T(1024)S(1)} %bitcast.289, bf16[48,1664]{1,0:T(8,128)(2,1)S(1)} %concatenate.21, ...), kind=kOutput, calls=%fused_computation.54.clone.1 | convolution fusion | flops 491762624 | bytes 11293060 | tf_op jit(solution)/shard_map/while/body/eval_jaxpr/dot_general | solution.py:126
  592.9 6.7 collective-permute-done.1
  601.8 6.7 convolution_convert_fusion.5
  611.1 10.2 %all-gather.6 = bf16[192,1664]{1,0:T(8,128)(2,1)S(1)} all-gather(bf16[48,1664]{1,0:T(8,128)(2,1)S(1)} %get-tuple-element.1050), channel_id=2, replica_groups=mesh['groups'=2,'section'=4,'dp'=4] {'dp'}, dimensions={0}, use_global_device_ids=true | all-gather | bytes 798720 | tf_op jit(solution)/shard_map/while/body/eval_jaxpr/all_gather | solution.py:228
  624.7 7.2 %fusion.108 = (f32[3072]{0:T(1024)S(1)}, f32[48]{0:T(128)S(1)}, f32[48,3072]{1,0:T(8,128)S(1)}) fusion(f32[48]{0:T(128)S(1)} %get-tuple-element.966, bf16[4,1,48,3072]{3,2,1,0:T(8,128)(2,1)} %get-tuple-element.1078, s32[]{:T(128)S(6)} %min.23, f32[3072]{0:T(1024)S(1)} %bitcast.289, bf16[48,1664]{1,0:T(8,128)(2,1)S(1)} %concatenate.21, ...), kind=kOutput, calls=%fused_computation.54.clone.1 | convolution fusion | flops 491762624 | bytes 11293060 | tf_op jit(solution)/shard_map/while/body/eval_jaxpr/dot_general | solution.py:126
  637.9 6.7 collective-permute-done.1
  644.5 7.1 %all-gather.2 = bf16[192,1664]{1,0:T(8,128)(2,1)S(1)} all-gather(bf16[48,1664]{1,0:T(8,128)(2,1)S(1)} %get-tuple-element.640), channel_id=4, replica_groups=mesh['groups'=2,'section'=4,'dp'=4] {'dp'}, dimensions={0}, use_global_device_ids=true | all-gather | bytes 798720 | tf_op jit(solution)/shard_map/all_gather | solution.py:259
  (400 shorter events, 325.5 us)
Async XLA Ops:
  7.2 170.3 %all-gather.10.cloned.1.call-start = ((), (), s32[]{:S(2)}) async-start(), calls=%async_computation | async-start | bytes 11796480 | tf_op jit(solution)/shard_map/all_gather | solution.py:147
  7.9 95.6 %collective-permute-start.2 = (bf16[768,1664]{1,0:T(8,128)(2,1)}, bf16[768,1664]{1,0:T(8,128)(2,1)S(1)}, u32[]{:S(2)}, u32[]{:S(2)}) collective-permute-start(bf16[768,1664]{1,0:T(8,128)(2,1)} %bitcast.283), channel_id=1, source_target_pairs={{0,1},{1,2},{2,3},{3,0},{4,5},{5,6},{6,7},{7,4},{8,9},{9,10},{10,1... | collective-permute-start | bytes 7667720 | tf_op jit(solution)/shard_map/ppermute | solution.py:25
  8.4 103.4 %collective-permute-start.4 = (bf16[768,1664]{1,0:T(8,128)(2,1)}, bf16[768,1664]{1,0:T(8,128)(2,1)}, u32[]{:S(2)}, u32[]{:S(2)}) collective-permute-start(bf16[768,1664]{1,0:T(8,128)(2,1)} %bitcast.284), channel_id=1, source_target_pairs={{1,0},{2,1},{3,2},{0,3},{5,4},{6,5},{7,6},{4,7},{9,8},{10,9},{11,1... | collective-permute-start | bytes 7667720 | tf_op jit(solution)/shard_map/ppermute | solution.py:27
  103.5 41.1 %collective-permute-start.3 = (bf16[768,1664]{1,0:T(8,128)(2,1)S(1)}, bf16[768,1664]{1,0:T(8,128)(2,1)}, u32[]{:S(2)}, u32[]{:S(2)}) collective-permute-start(bf16[768,1664]{1,0:T(8,128)(2,1)S(1)} %collective-permute-done.2), channel_id=1, source_target_pairs={{0,1},{1,2},{2,3},{3,0},{4,5},{5,6},{6,7},{7,4},{8,9},{9,10},{10,1... | collective-permute-start | bytes 7667720 | tf_op jit(solution)/shard_map/ppermute | solution.py:25
  203.7 10.1 %collective-permute-start = (bf16[1,48,3072]{2,1,0:T(8,128)(2,1)}, bf16[1,48,3072]{2,1,0:T(8,128)(2,1)}, u32[]{:S(2)}, u32[]{:S(2)}) collective-permute-start(bf16[1,48,3072]{2,1,0:T(8,128)(2,1)} %fusion.92), channel_id=1, source_target_pairs={{0,4},{4,8},{8,12},{1,5},{5,9},{9,13},{2,6},{6,10},{10,14},{3,7},{... | collective-permute-start | bytes 884744 | tf_op jit(solution)/shard_map/while/body/eval_jaxpr/ppermute | solution.py:37
  234.5 9.3 %collective-permute-start = (bf16[1,48,3072]{2,1,0:T(8,128)(2,1)}, bf16[1,48,3072]{2,1,0:T(8,128)(2,1)}, u32[]{:S(2)}, u32[]{:S(2)}) collective-permute-start(bf16[1,48,3072]{2,1,0:T(8,128)(2,1)} %fusion.92), channel_id=1, source_target_pairs={{0,4},{4,8},{8,12},{1,5},{5,9},{9,13},{2,6},{6,10},{10,14},{3,7},{... | collective-permute-start | bytes 884744 | tf_op jit(solution)/shard_map/while/body/eval_jaxpr/ppermute | solution.py:37
  264.5 9.3 %collective-permute-start = (bf16[1,48,3072]{2,1,0:T(8,128)(2,1)}, bf16[1,48,3072]{2,1,0:T(8,128)(2,1)}, u32[]{:S(2)}, u32[]{:S(2)}) collective-permute-start(bf16[1,48,3072]{2,1,0:T(8,128)(2,1)} %fusion.92), channel_id=1, source_target_pairs={{0,4},{4,8},{8,12},{1,5},{5,9},{9,13},{2,6},{6,10},{10,14},{3,7},{... | collective-permute-start | bytes 884744 | tf_op jit(solution)/shard_map/while/body/eval_jaxpr/ppermute | solution.py:37
  294.4 9.0 %collective-permute-start = (bf16[1,48,3072]{2,1,0:T(8,128)(2,1)}, bf16[1,48,3072]{2,1,0:T(8,128)(2,1)}, u32[]{:S(2)}, u32[]{:S(2)}) collective-permute-start(bf16[1,48,3072]{2,1,0:T(8,128)(2,1)} %fusion.92), channel_id=1, source_target_pairs={{0,4},{4,8},{8,12},{1,5},{5,9},{9,13},{2,6},{6,10},{10,14},{3,7},{... | collective-permute-start | bytes 884744 | tf_op jit(solution)/shard_map/while/body/eval_jaxpr/ppermute | solution.py:37
  324.0 9.0 %collective-permute-start = (bf16[1,48,3072]{2,1,0:T(8,128)(2,1)}, bf16[1,48,3072]{2,1,0:T(8,128)(2,1)}, u32[]{:S(2)}, u32[]{:S(2)}) collective-permute-start(bf16[1,48,3072]{2,1,0:T(8,128)(2,1)} %fusion.92), channel_id=1, source_target_pairs={{0,4},{4,8},{8,12},{1,5},{5,9},{9,13},{2,6},{6,10},{10,14},{3,7},{... | collective-permute-start | bytes 884744 | tf_op jit(solution)/shard_map/while/body/eval_jaxpr/ppermute | solution.py:37
  353.6 9.0 %collective-permute-start = (bf16[1,48,3072]{2,1,0:T(8,128)(2,1)}, bf16[1,48,3072]{2,1,0:T(8,128)(2,1)}, u32[]{:S(2)}, u32[]{:S(2)}) collective-permute-start(bf16[1,48,3072]{2,1,0:T(8,128)(2,1)} %fusion.92), channel_id=1, source_target_pairs={{0,4},{4,8},{8,12},{1,5},{5,9},{9,13},{2,6},{6,10},{10,14},{3,7},{... | collective-permute-start | bytes 884744 | tf_op jit(solution)/shard_map/while/body/eval_jaxpr/ppermute | solution.py:37
  364.8 306.0 %collective-permute-start.5 = (bf16[3,48,768]{2,1,0:T(8,128)(2,1)}, bf16[3,48,768]{2,1,0:T(8,128)(2,1)}, u32[]{:S(2)}, u32[]{:S(2)}) collective-permute-start(bf16[3,48,768]{2,1,0:T(8,128)(2,1)} %get-tuple-element.765), channel_id=1, source_target_pairs={{0,1},{1,2},{2,3},{3,0},{4,5},{5,6},{6,7},{7,4},{8,9},{9,10},{10,1... | collective-permute-start | bytes 663560 | tf_op jit(solution)/shard_map/ppermute | solution.py:160
  364.8 307.0 %collective-permute-start.6 = (bf16[3,48,768]{2,1,0:T(8,128)(2,1)}, bf16[3,48,768]{2,1,0:T(8,128)(2,1)}, u32[]{:S(2)}, u32[]{:S(2)}) collective-permute-start(bf16[3,48,768]{2,1,0:T(8,128)(2,1)} %get-tuple-element.764), channel_id=1, source_target_pairs={{0,2},{1,3},{2,0},{3,1},{4,6},{5,7},{6,4},{7,5},{8,10},{9,11},{10,... | collective-permute-start | bytes 663560 | tf_op jit(solution)/shard_map/ppermute | solution.py:160
  365.0 307.7 %collective-permute-start.7 = (bf16[3,48,768]{2,1,0:T(8,128)(2,1)}, bf16[3,48,768]{2,1,0:T(8,128)(2,1)}, u32[]{:S(2)}, u32[]{:S(2)}) collective-permute-start(bf16[3,48,768]{2,1,0:T(8,128)(2,1)} %get-tuple-element.763), channel_id=1, source_target_pairs={{0,3},{1,0},{2,1},{3,2},{4,7},{5,4},{6,5},{7,6},{8,11},{9,8},{10,9... | collective-permute-start | bytes 663560 | tf_op jit(solution)/shard_map/ppermute | solution.py:160
  371.8 24.2 %copy-start.1 = (f32[4,1,24,48,48]{3,4,2,1,0:T(8,128)}, f32[4,1,24,48,48]{3,4,2,1,0:T(8,128)S(1)}, u32[]{:S(2)}) copy-start(f32[4,1,24,48,48]{3,4,2,1,0:T(8,128)S(1)} %get-tuple-element.1080) | copy-start | bytes 2654212 | tf_op jit(solution)/shard_map/while
  371.8 37.3 %all-gather.12.cloned.1.call-start = ((), (), s32[]{:S(2)}) async-start(), calls=%async_computation.1 | async-start | bytes 1474560 | tf_op jit(solution)/shard_map/while/body/eval_jaxpr/all_gather | solution.py:227
  406.9 11.8 %collective-permute-start.1 = (bf16[1,48,3072]{2,1,0:T(8,128)(2,1)S(1)}, bf16[1,48,3072]{2,1,0:T(8,128)(2,1)}, u32[]{:S(2)}, u32[]{:S(2)}) collective-permute-start(bf16[1,48,3072]{2,1,0:T(8,128)(2,1)S(1)} %fusion.109), channel_id=1, source_target_pairs={{4,0},{8,4},{12,8},{5,1},{9,5},{13,9},{6,2},{10,6},{14,10},{7,3},{... | collective-permute-start | bytes 884744 | tf_op jit(solution)/shard_map/while/body/eval_jaxpr/ppermute | solution.py:37
  418.7 23.9 %copy-start.1 = (f32[4,1,24,48,48]{3,4,2,1,0:T(8,128)}, f32[4,1,24,48,48]{3,4,2,1,0:T(8,128)S(1)}, u32[]{:S(2)}) copy-start(f32[4,1,24,48,48]{3,4,2,1,0:T(8,128)S(1)} %get-tuple-element.1080) | copy-start | bytes 2654212 | tf_op jit(solution)/shard_map/while
  418.7 36.9 %all-gather.12.cloned.1.call-start = ((), (), s32[]{:S(2)}) async-start(), calls=%async_computation.1 | async-start | bytes 1474560 | tf_op jit(solution)/shard_map/while/body/eval_jaxpr/all_gather | solution.py:227
  453.4 11.3 %collective-permute-start.1 = (bf16[1,48,3072]{2,1,0:T(8,128)(2,1)S(1)}, bf16[1,48,3072]{2,1,0:T(8,128)(2,1)}, u32[]{:S(2)}, u32[]{:S(2)}) collective-permute-start(bf16[1,48,3072]{2,1,0:T(8,128)(2,1)S(1)} %fusion.109), channel_id=1, source_target_pairs={{4,0},{8,4},{12,8},{5,1},{9,5},{13,9},{6,2},{10,6},{14,10},{7,3},{... | collective-permute-start | bytes 884744 | tf_op jit(solution)/shard_map/while/body/eval_jaxpr/ppermute | solution.py:37
  464.7 36.0 %all-gather.12.cloned.1.call-start = ((), (), s32[]{:S(2)}) async-start(), calls=%async_computation.1 | async-start | bytes 1474560 | tf_op jit(solution)/shard_map/while/body/eval_jaxpr/all_gather | solution.py:227
  498.4 11.3 %collective-permute-start.1 = (bf16[1,48,3072]{2,1,0:T(8,128)(2,1)S(1)}, bf16[1,48,3072]{2,1,0:T(8,128)(2,1)}, u32[]{:S(2)}, u32[]{:S(2)}) collective-permute-start(bf16[1,48,3072]{2,1,0:T(8,128)(2,1)S(1)} %fusion.109), channel_id=1, source_target_pairs={{4,0},{8,4},{12,8},{5,1},{9,5},{13,9},{6,2},{10,6},{14,10},{7,3},{... | collective-permute-start | bytes 884744 | tf_op jit(solution)/shard_map/while/body/eval_jaxpr/ppermute | solution.py:37
  509.6 22.9 %copy-start.1 = (f32[4,1,24,48,48]{3,4,2,1,0:T(8,128)}, f32[4,1,24,48,48]{3,4,2,1,0:T(8,128)S(1)}, u32[]{:S(2)}) copy-start(f32[4,1,24,48,48]{3,4,2,1,0:T(8,128)S(1)} %get-tuple-element.1080) | copy-start | bytes 2654212 | tf_op jit(solution)/shard_map/while
  509.6 36.0 %all-gather.12.cloned.1.call-start = ((), (), s32[]{:S(2)}) async-start(), calls=%async_computation.1 | async-start | bytes 1474560 | tf_op jit(solution)/shard_map/while/body/eval_jaxpr/all_gather | solution.py:227
  543.3 11.3 %collective-permute-start.1 = (bf16[1,48,3072]{2,1,0:T(8,128)(2,1)S(1)}, bf16[1,48,3072]{2,1,0:T(8,128)(2,1)}, u32[]{:S(2)}, u32[]{:S(2)}) collective-permute-start(bf16[1,48,3072]{2,1,0:T(8,128)(2,1)S(1)} %fusion.109), channel_id=1, source_target_pairs={{4,0},{8,4},{12,8},{5,1},{9,5},{13,9},{6,2},{10,6},{14,10},{7,3},{... | collective-permute-start | bytes 884744 | tf_op jit(solution)/shard_map/while/body/eval_jaxpr/ppermute | solution.py:37
  554.6 35.9 %all-gather.12.cloned.1.call-start = ((), (), s32[]{:S(2)}) async-start(), calls=%async_computation.1 | async-start | bytes 1474560 | tf_op jit(solution)/shard_map/while/body/eval_jaxpr/all_gather | solution.py:227
  588.3 11.3 %collective-permute-start.1 = (bf16[1,48,3072]{2,1,0:T(8,128)(2,1)S(1)}, bf16[1,48,3072]{2,1,0:T(8,128)(2,1)}, u32[]{:S(2)}, u32[]{:S(2)}) collective-permute-start(bf16[1,48,3072]{2,1,0:T(8,128)(2,1)S(1)} %fusion.109), channel_id=1, source_target_pairs={{4,0},{8,4},{12,8},{5,1},{9,5},{13,9},{6,2},{10,6},{14,10},{7,3},{... | collective-permute-start | bytes 884744 | tf_op jit(solution)/shard_map/while/body/eval_jaxpr/ppermute | solution.py:37
  599.5 22.9 %copy-start.1 = (f32[4,1,24,48,48]{3,4,2,1,0:T(8,128)}, f32[4,1,24,48,48]{3,4,2,1,0:T(8,128)S(1)}, u32[]{:S(2)}) copy-start(f32[4,1,24,48,48]{3,4,2,1,0:T(8,128)S(1)} %get-tuple-element.1080) | copy-start | bytes 2654212 | tf_op jit(solution)/shard_map/while
  599.6 35.9 %all-gather.12.cloned.1.call-start = ((), (), s32[]{:S(2)}) async-start(), calls=%async_computation.1 | async-start | bytes 1474560 | tf_op jit(solution)/shard_map/while/body/eval_jaxpr/all_gather | solution.py:227
  633.3 11.3 %collective-permute-start.1 = (bf16[1,48,3072]{2,1,0:T(8,128)(2,1)S(1)}, bf16[1,48,3072]{2,1,0:T(8,128)(2,1)}, u32[]{:S(2)}, u32[]{:S(2)}) collective-permute-start(bf16[1,48,3072]{2,1,0:T(8,128)(2,1)S(1)} %fusion.109), channel_id=1, source_target_pairs={{4,0},{8,4},{12,8},{5,1},{9,5},{13,9},{6,2},{10,6},{14,10},{7,3},{... | collective-permute-start | bytes 884744 | tf_op jit(solution)/shard_map/while/body/eval_jaxpr/ppermute | solution.py:37
  652.8 8.4 %collective-permute-start.8 = (bf16[3,48,384]{2,1,0:T(8,128)(2,1)S(1)}, bf16[3,48,384]{2,1,0:T(8,128)(2,1)S(1)}, u32[]{:S(2)}, u32[]{:S(2)}) collective-permute-start(bf16[3,48,384]{2,1,0:T(8,128)(2,1)S(1)} %get-tuple-element.769), channel_id=1, source_target_pairs={{0,1},{1,2},{2,3},{3,0},{4,5},{5,6},{6,7},{7,4},{8,9},{9,10},{10,1... | collective-permute-start | bytes 331784 | tf_op jit(solution)/shard_map/ppermute | solution.py:160
  653.2 8.9 %collective-permute-start.9 = (bf16[3,48,384]{2,1,0:T(8,128)(2,1)S(1)}, bf16[3,48,384]{2,1,0:T(8,128)(2,1)S(1)}, u32[]{:S(2)}, u32[]{:S(2)}) collective-permute-start(bf16[3,48,384]{2,1,0:T(8,128)(2,1)S(1)} %get-tuple-element.768), channel_id=1, source_target_pairs={{0,2},{1,3},{2,0},{3,1},{4,6},{5,7},{6,4},{7,5},{8,10},{9,11},{10,... | collective-permute-start | bytes 331784 | tf_op jit(solution)/shard_map/ppermute | solution.py:160
  661.2 3.2 collective-permute-start.10
  (38 other events, 214.8 us)
Sparse Core Ops, SparseCore 0:
  9.6 113.8 all-gather.9
  374.2 22.8 all-gather.11
  421.1 20.8 all-gather.11
  467.0 19.3 all-gather.11
  512.0 19.3 all-gather.11
  557.0 19.3 all-gather.11
  601.9 19.4 all-gather.11
